TPU v7x, 32 devices: a whole 2x2x4 slice. The times are simulated.
32 devices in a mesh: tower: 2 (over core), batch: 16 (over z, y, x).
Axes of the slice: x: 2, y: 2, z: 4, core: 2. Of those that a mesh axis runs over, the one named last changes fastest.
Arguments:
- tokens: bfloat16 [2, 32768, 768], P('tower', 'batch'), may hold values from -6 to 6
- lengths: int32 [2, 64], P('tower', 'batch'), may hold values from 64 to 512, as said below
- prefixes: int32 [2, 64], P('tower', 'batch'), may hold values from 1 to 32
- positives: int32 [64], replicated, may hold values from 0 to 63, each once
- gain_attention: float32 [768], replicated, may hold values from 0.5 to 1.5
- query_weight: bfloat16 [768, 768], replicated, may hold values from -0.02734375 to 0.02734375
- key_weight: bfloat16 [768, 768], replicated, may hold values from -0.21875 to 0.21875
- value_weight: bfloat16 [768, 768], replicated, may hold values from -0.21875 to 0.21875
- output_weight: bfloat16 [768, 768], replicated, may hold values from -1.75 to 1.75
- bucket_bias: float32 [32, 12], replicated, may hold values from -4 to 4
- gain_feedforward: float32 [768], replicated, may hold values from 0.5 to 1.5
- widen_weight: bfloat16 [768, 3072], replicated, may hold values from -0.21875 to 0.21875
- narrow_weight: bfloat16 [3072, 768], replicated, may hold values from -0.109375 to 0.109375
- gain_final: float32 [768], replicated, may hold values from 0.5 to 1.5
Outputs:
- contrast_loss: float32 [], replicated
- score_gradient: float32 [64, 64], P('batch')
- token_gradient: bfloat16 [2, 32768, 768], P('tower', 'batch')
- grad_attention: float32 [768], replicated
- grad_query: float32 [768, 768], replicated
- grad_key: float32 [768, 768], replicated
- grad_value: float32 [768, 768], replicated
- grad_output: float32 [768, 768], replicated
- grad_bucket: float32 [32, 12], replicated
- grad_feedforward: float32 [768], replicated
- grad_widen: float32 [768, 3072], replicated
- grad_narrow: float32 [3072, 768], replicated
- grad_final: float32 [768], replicated
Inputs may be any that keep to these rules, and one draw needn't show every extreme that they name: `lengths`: sequence 0 of each side uses all 512 positions. `positives`: every document is the positive of exactly one query.
All inputs are finite; a program needn't handle non-finite values.
Results may differ from a plain program's by a relative error of at most 0.025.
The roundings to bfloat16 on the way count: a program that leaves them out, or rounds other values in their place, can miss the bound.
Values sent between devices are 32-bit elements; how exact they have to be, the bound alone decides.
A program may use at most 320 MiB of HBM per device.

v0:
```python
import jax
import jax.numpy as jnp
from jax import lax
from jax.sharding import PartitionSpec as P

epsilon = 1e-06
masked_score = -1000000000.0
score_scale = 100.0
far_steps = (12, 16, 23, 32, 46, 64, 91)
highest = lax.Precision.HIGHEST


def bucket_onehot(slot_len, bucket_count):
    places = jnp.arange(slot_len, dtype=jnp.int32)
    offset = places[None, :] - places[:, None]
    spread = jnp.abs(offset)
    far_bucket = 8 + sum(((spread >= step).astype(jnp.int32) for step in far_steps))
    bucket = jnp.where(spread < 8, spread, far_bucket) + jnp.where(
        offset > 0, bucket_count // 2, 0
    ).astype(jnp.int32)
    labels = jnp.arange(bucket_count, dtype=jnp.int32)
    return (bucket[:, :, None] == labels[None, None, :]).astype(jnp.float32)


def norm_forward(values, scale_vec):
    inverse = lax.rsqrt(jnp.mean(values * values, axis=-1, keepdims=True) + epsilon)
    return (values * inverse * scale_vec, inverse)


def norm_backward(values, inverse, scale_vec, upstream):
    scaled = upstream * scale_vec
    inner_mean = jnp.mean(scaled * values, axis=-1, keepdims=True)
    grad_values = inverse * scaled - values * (inverse * inverse * inverse) * inner_mean
    grad_scale = jnp.sum(upstream * values * inverse, axis=0)
    return (grad_values, grad_scale)


def local(
    tokens,
    lengths,
    prefixes,
    positives,
    gain_attention,
    query_weight,
    key_weight,
    value_weight,
    output_weight,
    bucket_bias,
    gain_feedforward,
    widen_weight,
    narrow_weight,
    gain_final,
):
    seqs = lengths.shape[1]
    rows = tokens.shape[1]
    slot_len = rows // seqs
    width = tokens.shape[2]
    heads = bucket_bias.shape[1]
    head_dim = query_weight.shape[1] // heads
    inner = heads * head_dim
    tokens_f = tokens[0].astype(jnp.float32)
    seq_lengths = lengths[0]
    seq_prefix = prefixes[0]
    onehot = bucket_onehot(slot_len, bucket_bias.shape[0])
    bias = jnp.einsum("ijb,bh->hij", onehot, bucket_bias, precision=highest)
    normed_f, inverse_first = norm_forward(tokens_f, gain_attention)
    normed = normed_f.astype(jnp.bfloat16)

    def project(matrix):
        projected = jnp.dot(normed, matrix, preferred_element_type=jnp.float32).astype(jnp.bfloat16)
        return projected.reshape(seqs, slot_len, heads, head_dim)

    query_all = project(query_weight)
    key_all = project(key_weight)
    value_all = project(value_weight)
    places = jnp.arange(slot_len, dtype=jnp.int32)
    valid = places[None, :] < seq_lengths[:, None]

    def score_block(query_rows, key_rows, valid_keys):
        raw_scores = jnp.einsum(
            "ihd,jhd->hij", query_rows, key_rows, preferred_element_type=jnp.float32
        )
        return jnp.where(valid_keys[None, None, :], raw_scores + bias, masked_score)

    def attend_forward(parts):
        query_rows, key_rows, value_rows, valid_keys = parts
        scores = score_block(query_rows, key_rows, valid_keys)
        row_peak = jnp.max(scores, axis=-1, keepdims=True)
        raised = jnp.exp(scores - row_peak)
        totals = jnp.sum(raised, axis=-1, keepdims=True)
        soft_low = (raised / totals).astype(jnp.bfloat16)
        context = jnp.einsum(
            "hij,jhd->ihd", soft_low, value_rows, preferred_element_type=jnp.float32
        )
        return (context.astype(jnp.bfloat16), (row_peak + jnp.log(totals))[:, :, 0])

    context, log_totals = lax.map(attend_forward, (query_all, key_all, value_all, valid))
    context_flat = context.reshape(rows, inner)
    mixed = tokens_f + jnp.dot(context_flat, output_weight, preferred_element_type=jnp.float32)
    ffn_in_f, inverse_second = norm_forward(mixed, gain_feedforward)
    ffn_in = ffn_in_f.astype(jnp.bfloat16)
    pre_act = jnp.dot(ffn_in, widen_weight, preferred_element_type=jnp.float32)
    hidden = jnp.where(pre_act > 0, pre_act, 0.0).astype(jnp.bfloat16)
    output = mixed + jnp.dot(hidden, narrow_weight, preferred_element_type=jnp.float32)
    final, inverse_third = norm_forward(output, gain_final)
    pool_mask = ((places[None, :] >= seq_prefix[:, None]) & valid).astype(jnp.float32)
    pool_weight = pool_mask / jnp.sum(pool_mask, axis=1, keepdims=True)
    pooled = jnp.sum(final.reshape(seqs, slot_len, width) * pool_weight[:, :, None], axis=1)
    inverse_pool = lax.rsqrt(jnp.sum(pooled * pooled, axis=-1, keepdims=True) + epsilon)
    unit = pooled * inverse_pool
    gathered = lax.all_gather(unit, ("tower", "batch"), axis=0, tiled=True)
    total_seqs = gathered.shape[0] // 2
    query_units = gathered[:total_seqs]
    doc_units = gathered[total_seqs:]
    scores = score_scale * jnp.dot(query_units, doc_units.T, precision=highest)
    labels = jnp.arange(total_seqs, dtype=jnp.int32)
    target = (positives[:, None] == labels[None, :]).astype(jnp.float32)
    row_peak = jnp.max(scores, axis=1, keepdims=True)
    row_raised = jnp.exp(scores - row_peak)
    row_sum = jnp.sum(row_raised, axis=1, keepdims=True)
    col_peak = jnp.max(scores, axis=0, keepdims=True)
    col_raised = jnp.exp(scores - col_peak)
    col_sum = jnp.sum(col_raised, axis=0, keepdims=True)
    loss_value = (
        0.5 * jnp.sum(row_peak[:, 0] + jnp.log(row_sum[:, 0]))
        + 0.5 * jnp.sum(col_peak[0] + jnp.log(col_sum[0]))
        - jnp.sum(target * scores)
    )
    score_grad = 0.5 * row_raised / row_sum + 0.5 * col_raised / col_sum - target
    tower = lax.axis_index("tower")
    first_row = lax.axis_index("batch") * seqs
    my_rows = lax.dynamic_slice_in_dim(score_grad, first_row, seqs, 0)
    my_cols = lax.dynamic_slice_in_dim(score_grad, first_row, seqs, 1)
    grad_as_query = score_scale * jnp.dot(my_rows, doc_units, precision=highest)
    grad_as_doc = score_scale * jnp.dot(my_cols.T, query_units, precision=highest)
    grad_unit = jnp.where(tower == 0, grad_as_query, grad_as_doc)
    cubed = inverse_pool * inverse_pool * inverse_pool
    grad_pooled = inverse_pool * grad_unit - pooled * cubed * jnp.sum(
        grad_unit * pooled, axis=-1, keepdims=True
    )
    grad_fin = (pool_weight[:, :, None] * grad_pooled[:, None, :]).reshape(rows, width)
    grad_out, grad_final = norm_backward(output, inverse_third, gain_final, grad_fin)
    grad_branch = grad_out.astype(jnp.bfloat16)
    grad_narrow = jnp.einsum("tf,td->fd", hidden, grad_branch, preferred_element_type=jnp.float32)
    grad_hidden = jnp.einsum(
        "td,fd->tf", grad_branch, narrow_weight, preferred_element_type=jnp.float32
    )
    grad_pre = jnp.where(pre_act > 0, grad_hidden, 0.0).astype(jnp.bfloat16)
    grad_widen = jnp.einsum("td,tf->df", ffn_in, grad_pre, preferred_element_type=jnp.float32)
    grad_ffn_in = jnp.einsum(
        "tf,df->td", grad_pre, widen_weight, preferred_element_type=jnp.float32
    )
    grad_mixed_norm, grad_feedforward = norm_backward(
        mixed, inverse_second, gain_feedforward, grad_ffn_in
    )
    grad_mixed = grad_out + grad_mixed_norm
    grad_attn = grad_mixed.astype(jnp.bfloat16)
    grad_output = jnp.einsum(
        "ti,td->id", context_flat, grad_attn, preferred_element_type=jnp.float32
    )
    grad_context = jnp.einsum(
        "td,id->ti", grad_attn, output_weight, preferred_element_type=jnp.float32
    )
    grad_context = grad_context.astype(jnp.bfloat16).reshape(seqs, slot_len, heads, head_dim)

    def attend_backward(bias_total, parts):
        query_rows, key_rows, value_rows, valid_keys, log_rows, context_grad = parts
        scores_here = score_block(query_rows, key_rows, valid_keys)
        soft = jnp.exp(scores_here - log_rows[:, :, None])
        soft_low = soft.astype(jnp.bfloat16)
        value_part = jnp.einsum(
            "hij,ihd->jhd", soft_low, context_grad, preferred_element_type=jnp.float32
        )
        grad_soft = jnp.einsum(
            "ihd,jhd->hij", context_grad, value_rows, preferred_element_type=jnp.float32
        )
        grad_scores = soft * (grad_soft - jnp.sum(grad_soft * soft, axis=-1, keepdims=True))
        scores_low = grad_scores.astype(jnp.bfloat16)
        query_part = jnp.einsum(
            "hij,jhd->ihd", scores_low, key_rows, preferred_element_type=jnp.float32
        )
        key_part = jnp.einsum(
            "hij,ihd->jhd", scores_low, query_rows, preferred_element_type=jnp.float32
        )
        return (
            bias_total + grad_scores,
            (
                query_part.astype(jnp.bfloat16),
                key_part.astype(jnp.bfloat16),
                value_part.astype(jnp.bfloat16),
            ),
        )

    bias_total, (query_grads, key_grads, value_grads) = lax.scan(
        attend_backward,
        jnp.zeros(bias.shape, jnp.float32),
        (query_all, key_all, value_all, valid, log_totals, grad_context),
    )
    query_grads = query_grads.reshape(rows, inner)
    key_grads = key_grads.reshape(rows, inner)
    value_grads = value_grads.reshape(rows, inner)
    grad_bucket = jnp.einsum("ijb,hij->bh", onehot, bias_total, precision=highest)
    grad_query = jnp.einsum("td,ti->di", normed, query_grads, preferred_element_type=jnp.float32)
    grad_key = jnp.einsum("td,ti->di", normed, key_grads, preferred_element_type=jnp.float32)
    grad_value = jnp.einsum("td,ti->di", normed, value_grads, preferred_element_type=jnp.float32)
    grad_normed = (
        jnp.einsum("ti,di->td", query_grads, query_weight, preferred_element_type=jnp.float32)
        + jnp.einsum("ti,di->td", key_grads, key_weight, preferred_element_type=jnp.float32)
        + jnp.einsum("ti,di->td", value_grads, value_weight, preferred_element_type=jnp.float32)
    )
    grad_tokens_norm, grad_attention = norm_backward(
        tokens_f, inverse_first, gain_attention, grad_normed
    )
    token_gradient = (grad_mixed + grad_tokens_norm).astype(jnp.bfloat16)[None]
    (
        sum_attention,
        sum_query,
        sum_key,
        sum_value,
        sum_output,
        sum_bucket,
        sum_feedforward,
        sum_widen,
        sum_narrow,
        sum_final,
    ) = lax.psum(
        (
            grad_attention,
            grad_query,
            grad_key,
            grad_value,
            grad_output,
            grad_bucket,
            grad_feedforward,
            grad_widen,
            grad_narrow,
            grad_final,
        ),
        ("tower", "batch"),
    )
    return (
        loss_value,
        my_rows,
        token_gradient,
        sum_attention,
        sum_query,
        sum_key,
        sum_value,
        sum_output,
        sum_bucket,
        sum_feedforward,
        sum_widen,
        sum_narrow,
        sum_final,
    )


def solution(mesh):
    placed = (
        P("tower", "batch", None),
        P("tower", "batch"),
        P("tower", "batch"),
        P(),
        P(),
        P(),
        P(),
        P(),
        P(),
        P(),
        P(),
        P(),
        P(),
        P(),
    )
    return jax.shard_map(
        local,
        mesh=mesh,
        in_specs=placed,
        out_specs=(
            P(),
            P("batch", None),
            P("tower", "batch", None),
            P(),
            P(),
            P(),
            P(),
            P(),
            P(),
            P(),
            P(),
            P(),
            P(),
        ),
        check_vma=False,
    )
```

profile of v0, /device:TPU:0, one launch (start us, length us, event | category | flops | bytes accessed | tf_op | source)
XLA Modules:
  0.0 1078.6 jit_solution(5208512605683882147)
XLA Ops:
  74.6 13.7 %fusion.55 = f32[12,512,512]{2,0,1:T(8,128)} fusion(s32[512,512]{1,0:T(8,128)S(1)} %fusion.93, f32[32,12]{0,1:T(8,128)S(1)} %copy-done.36), kind=kOutput, calls=%fused_computation.65 | convolution fusion | flops 1216348160 | bytes 13633024 | tf_op jit(solution)/shard_map/ijb,bh->hij/dot_general | solution.py:65
  88.2 17.3 %copy.73 = f32[12,512,512]{1,2,0:T(8,128)} copy(f32[12,512,512]{2,0,1:T(8,128)} %fusion.55) | data formatting | bytes 25165824 | tf_op jit(solution)/shard_map/while | solution.py:97
  107.6 59.8 %while.29 = (s32[]{:T(128)}, bf16[4,512,12,64]{1,3,2,0:T(8,128)(2,1)}, f32[4,12,512]{2,1,0:T(8,128)}, bf16[4,512,12,64]{1,3,2,0:T(8,128)(2,1)}, pred[4,512]{1,0:...) while((s32[]{:T(128)}, ...), condition=%wide.region_4.5_spmd, body=%wide.region_1.4_spmd.sunk | while | flops 830859264 | bytes 53685868 | solution.py:97
  179.0 13.7 %fusion.113 = f32[2048,3072]{1,0:T(8,128)} fusion(bf16[768,3072]{1,0:T(8,128)(2,1)S(1)} %bitcast.270, f32[2048,768]{1,0:T(8,128)S(1)} %get-tuple-element.306, f32[768]{0:T(1024)S(1)} %copy-done.46, f32[2048]{0:T(1024)S(1)} %get-tuple-element.298), kind=kOutput, calls=%fused_computation.170 | convolution fusion | flops 9668395008 | bytes 36187136 | tf_op jit(solution)/shard_map/dot_general | solution.py:102
  192.7 19.2 %multiply_reduce_fusion.4 = (f32[2048]{0:T(1024)S(1)}, f32[2048,768]{1,0:T(8,128)}) fusion(f32[2048,768]{1,0:T(8,128)} %copy-done.16, bf16[3072,768]{1,0:T(8,128)(2,1)} %param.30, f32[2048,3072]{1,0:T(8,128)} %fusion.113), kind=kOutput, calls=%fused_computation.101 | convolution fusion | flops 9687267328 | bytes 42475520 | tf_op jit(solution)/shard_map/dot_general | solution.py:104
  215.5 72.1 %all-gather = f32[32,4,768]{2,1,0:T(4,128)S(1)} all-gather(f32[1,4,768]{2,1,0:T(4,128)S(1)} %multiply_bitcast_fusion), channel_id=1, replica_groups=mesh['tower'=2,'batch'=16] {'tower','batch'}, dimensions={0}, use_global_device_ids=true | all-gather | bytes 405504 | tf_op jit(solution)/shard_map/all_gather | solution.py:111
  300.3 18.3 %fusion.83 = f32[3072,768]{1,0:T(8,128)} fusion(bf16[2048,768]{1,0:T(8,128)(2,1)} %fusion.82, f32[2048,3072]{1,0:T(8,128)} %fusion.113), kind=kOutput, calls=%fused_computation.110 | convolution fusion | flops 9682550784 | bytes 37748736 | tf_op jit(solution)/shard_map/tf,td->fd/dot_general | solution.py:144
  318.5 20.8 %fusion.52 = bf16[2048,3072]{1,0:T(8,128)(2,1)} fusion(f32[2048,3072]{1,0:T(8,128)} %fusion.113, bf16[2048,768]{1,0:T(8,128)(2,1)} %fusion.82, bf16[3072,768]{1,0:T(8,128)(2,1)} %param.30), kind=kOutput, calls=%fused_computation.62 | convolution fusion | flops 9682550784 | bytes 45613056 | tf_op jit(solution)/shard_map/td,fd->tf/dot_general | solution.py:145
  339.4 17.4 %multiply_reduce_fusion.1 = (f32[768]{0:T(1024)}, f32[2048]{0:T(1024)S(1)}, f32[2048,768]{1,0:T(8,128)}) fusion(f32[2048,768]{1,0:T(8,128)S(1)} %bitcast.254, f32[2048]{0:T(1024)S(1)} %get-tuple-element.298, f32[768]{0:T(1024)S(1)} %copy-done.46, bf16[2048,3072]{1,0:T(8,128)(2,1)} %fusion.52, bf16[768,3072]{1,0:T(8,128)(2,1)} %param.29), kind=kOutput, calls=%fused_computation.95 | convolution fusion | flops 9673110528 | bytes 29906944 | tf_op jit(solution)/shard_map/tf,df->td/dot_general | solution.py:150
  356.8 15.6 %fusion.112 = f32[768,3072]{1,0:T(8,128)} fusion(bf16[2048,3072]{1,0:T(8,128)(2,1)} %fusion.52, f32[2048,768]{1,0:T(8,128)S(1)} %bitcast.254, f32[768]{0:T(1024)S(1)} %copy-done.46, f32[2048]{0:T(1024)S(1)} %get-tuple-element.298), kind=kOutput, calls=%fused_computation.169 | convolution fusion | flops 9668395008 | bytes 28322816 | tf_op jit(solution)/shard_map/td,tf->df/dot_general | solution.py:149
  405.7 183.0 %while.30 = (s32[]{:T(128)}, f32[12,512,512]{1,2,0:T(8,128)}, bf16[4,512,12,64]{1,3,2,0:T(8,128)(2,1)}, bf16[4,512,12,64]{1,3,2,0:T(8,128)(2,1)}, bf16[4,512,12,...) while((s32[]{:T(128)}, f32[12,512,512]{1,2,0:T(8,128)}, ...), condition=%wide.region_22.23_spmd.clone, body=%wide.region_20.22_spmd.clone.sunk | while | flops 2049042432 | bytes 177863392 | solution.py:194
  406.5 8.8 subtract_exponential_fusion.5
  425.8 13.5 %fusion.188 = (bf16[12,512,512]{1,2,0:T(8,128)(2,1)}, f32[12,512,512]{1,2,0:T(8,128)}) fusion(f32[12,512,512]{1,2,0:T(8,128)S(1)} %subtract_exponential_fusion.5, f32[12,512,512]{1,2,0:T(8,128)} %get-tuple-element.446, f32[12,512]{1,0:T(8,128)S(1)} %get-tuple-element.447, f32[12,512,512]{1,2,0:T(8,128)} %get-tuple-element.492, pred[]{:T(512)S(6)} %compare.3), kind=kLoop, calls=%fused_computation.24.clone.1 | loop fusion | flops 15728640 | bytes 56647680 | tf_op jit(solution)/shard_map/while/body/eval_jaxpr/convert_element_type | solution.py:178
  449.3 8.8 subtract_exponential_fusion.5
  468.6 17.4 %fusion.188 = (bf16[12,512,512]{1,2,0:T(8,128)(2,1)}, f32[12,512,512]{1,2,0:T(8,128)}) fusion(f32[12,512,512]{1,2,0:T(8,128)S(1)} %subtract_exponential_fusion.5, f32[12,512,512]{1,2,0:T(8,128)} %get-tuple-element.446, f32[12,512]{1,0:T(8,128)S(1)} %get-tuple-element.447, f32[12,512,512]{1,2,0:T(8,128)} %get-tuple-element.492, pred[]{:T(512)S(6)} %compare.3), kind=kLoop, calls=%fused_computation.24.clone.1 | loop fusion | flops 15728640 | bytes 56647680 | tf_op jit(solution)/shard_map/while/body/eval_jaxpr/convert_element_type | solution.py:178
  515.3 17.4 %fusion.188 = (bf16[12,512,512]{1,2,0:T(8,128)(2,1)}, f32[12,512,512]{1,2,0:T(8,128)}) fusion(f32[12,512,512]{1,2,0:T(8,128)S(1)} %subtract_exponential_fusion.5, f32[12,512,512]{1,2,0:T(8,128)} %get-tuple-element.446, f32[12,512]{1,0:T(8,128)S(1)} %get-tuple-element.447, f32[12,512,512]{1,2,0:T(8,128)} %get-tuple-element.492, pred[]{:T(512)S(6)} %compare.3), kind=kLoop, calls=%fused_computation.24.clone.1 | loop fusion | flops 15728640 | bytes 56647680 | tf_op jit(solution)/shard_map/while/body/eval_jaxpr/convert_element_type | solution.py:178
  542.6 8.8 subtract_exponential_fusion.5
  561.9 17.4 %fusion.188 = (bf16[12,512,512]{1,2,0:T(8,128)(2,1)}, f32[12,512,512]{1,2,0:T(8,128)}) fusion(f32[12,512,512]{1,2,0:T(8,128)S(1)} %subtract_exponential_fusion.5, f32[12,512,512]{1,2,0:T(8,128)} %get-tuple-element.446, f32[12,512]{1,0:T(8,128)S(1)} %get-tuple-element.447, f32[12,512,512]{1,2,0:T(8,128)} %get-tuple-element.492, pred[]{:T(512)S(6)} %compare.3), kind=kLoop, calls=%fused_computation.24.clone.1 | loop fusion | flops 15728640 | bytes 56647680 | tf_op jit(solution)/shard_map/while/body/eval_jaxpr/convert_element_type | solution.py:178
  617.3 18.7 %copy.84 = f32[12,512,512]{2,0,1:T(8,128)} copy(f32[12,512,512]{1,2,0:T(8,128)} %get-tuple-element.126) | data formatting | bytes 25165824 | tf_op jit(solution)/shard_map/while | solution.py:194
  654.5 17.5 %fusion.92 = f32[32,12]{0,1:T(8,128)S(1)} fusion(f32[12,512,512]{2,0,1:T(8,128)S(1)} %copy-done.2, s32[512,512]{1,0:T(8,128)S(1)} %copy-done.11), kind=kOutput, calls=%fused_computation.121 | convolution fusion | flops 1216348160 | bytes 13633024 | tf_op jit(solution)/shard_map/ijb,hij->bh/dot_general | solution.py:202
  672.1 9.1 fusion.71
  681.2 39.6 %all-reduce = (f32[768]{0:T(1024)}, f32[32,12]{0,1:T(8,128)}, f32[768]{0:T(1024)}, f32[768]{0:T(1024)}) all-reduce(f32[768]{0:T(1024)S(1)} %get-tuple-element.228, f32[32,12]{0,1:T(8,128)S(1)} %fusion.92, f32[768]{0:T(1024)S(1)} %copy-done.47, f32[768]{0:T(1024)S(1)} %copy-done.33), channel_id=1, replica_groups=mesh['tower'=2,'batch'=16] {'tower','batch'}, use_global_device_ids=true, to_apply=%region_25.26 | all-reduce | flops 2688 | bytes 21504 | tf_op jit(solution)/shard_map/psum | solution.py:226
  729.1 320.5 %all-reduce.4.cloned.1.call-done = (f32[768,768]{1,0:T(8,128)}, f32[768,768]{1,0:T(8,128)}, f32[768,768]{1,0:T(8,128)}, f32[768,768]{1,0:T(8,128)}, f32[768,3072]{1,0:T(8,128)}, /*index=5*/f32[3072,768]{1,0:T(8,128)}) async-done(((f32[768,768]{1,0:T(8,128)}, f32[768,768]{1,0:T(8,128)}, f32[768,768]{1,0:T(8,128)}, f32[768,768]{1,0:T(8,128)}, f32[768,3072]{1,0:T(8,128)}, /*index=5*/f32[3072,768]{1,0:T(8,128)}), ...) | async-done | bytes 28311568 | tf_op jit(solution)/shard_map/psum | solution.py:226
  1057.3 9.3 copy.133
  (260 shorter events, 344.7 us)
Async XLA Ops:
  7.2 48.2 %copy-start = (bf16[768,768]{1,0:T(8,128)(2,1)S(1)}, bf16[768,768]{1,0:T(8,128)(2,1)}, u32[]{:S(2)}) copy-start(bf16[768,768]{1,0:T(8,128)(2,1)} %param.25) | copy-start | bytes 3538948
  7.2 1042.5 %all-reduce.4.cloned.1.call-start = ((), (), s32[]{:S(2)}) async-start(), calls=%async_computation | async-start | bytes 56623104 | tf_op jit(solution)/shard_map/psum | solution.py:226
  7.7 66.9 %copy-start.10 = (s32[512,512]{1,0:T(8,128)}, s32[512,512]{1,0:T(8,128)S(1)}, u32[]{:S(2)}) copy-start(s32[512,512]{1,0:T(8,128)S(1)} %fusion.93) | copy-start | bytes 3145732
  12.5 42.9 %copy-start.27 = (f32[2048]{0:T(1024)}, f32[2048]{0:T(1024)S(1)}, u32[]{:S(2)}) copy-start(f32[2048]{0:T(1024)S(1)} %get-tuple-element.296) | copy-start | bytes 24580
  25.4 10.7 copy-start.52
  192.7 19.2 %copy-start.29 = (f32[768]{0:T(1024)S(1)}, f32[768]{0:T(1024)}, u32[]{:S(2)}) copy-start(f32[768]{0:T(1024)} %param.31) | copy-start | bytes 9220
  192.7 19.2 %copy-start.31 = (f32[4,512]{1,0:T(4,128)S(1)}, f32[4,512]{1,0:T(4,128)}, u32[]{:S(2)}) copy-start(f32[4,512]{1,0:T(4,128)} %get-tuple-element.302) | copy-start | bytes 24580
  211.9 76.4 %copy-start.48 = (s32[64]{0:T(128)S(1)}, s32[64]{0:T(128)}, u32[]{:S(2)}) copy-start(s32[64]{0:T(128)} %param.21) | copy-start | bytes 772
  211.9 78.2 %copy-start.32 = (f32[1,4,4,128]{3,2,1,0:T(4,128)S(1)}, f32[1,4,4,128]{3,2,1,0:T(4,128)}, u32[]{:S(2)}) copy-start(f32[1,4,4,128]{3,2,1,0:T(4,128)} %get-tuple-element.301) | copy-start | bytes 24580
  295.3 44.0 %slice-start.5 = ((s8[6291456]{0:T(1024)(128)(4,1)}), s8[4194304]{0:T(1024)(128)(4,1)S(1)}, s32[]{:S(2)}) async-start(s8[6291456]{0:T(1024)(128)(4,1)} %bitcast.253), calls=%async_computation.6 | async-start | bytes 8388608
  300.3 39.1 %slice-start.6 = ((s8[6291456]{0:T(1024)(128)(4,1)}), s8[2097152]{0:T(1024)(128)(4,1)S(1)}, s32[]{:S(2)}) async-start(s8[6291456]{0:T(1024)(128)(4,1)} %bitcast.253), calls=%async_computation.7 | async-start | bytes 4194304
  318.5 53.8 %slice-start = ((s8[6291456]{0:T(1024)(128)(4,1)}), s8[2097152]{0:T(1024)(128)(4,1)S(1)}, s32[]{:S(2)}) async-start(s8[6291456]{0:T(1024)(128)(4,1)} %bitcast.243), calls=%async_computation.1 | async-start | bytes 4194304
  339.4 33.0 %slice-start.1 = ((s8[6291456]{0:T(1024)(128)(4,1)}), s8[4194304]{0:T(1024)(128)(4,1)S(1)}, s32[]{:S(2)}) async-start(s8[6291456]{0:T(1024)(128)(4,1)} %bitcast.243), calls=%async_computation.2 | async-start | bytes 8388608
  356.8 15.6 %copy-start.17 = (f32[2048,768]{1,0:T(8,128)S(1)}, f32[2048,768]{1,0:T(8,128)}, u32[]{:S(2)}) copy-start(f32[2048,768]{1,0:T(8,128)} %get-tuple-element.312) | copy-start | bytes 18874372
  617.2 18.7 %copy-start.38 = (f32[64]{0:T(128)S(1)}, f32[64]{0:T(128)}, u32[]{:S(2)}) copy-start(f32[64]{0:T(128)} %copy-done.37) | copy-start | bytes 772
  617.2 18.7 %copy-start.40 = (f32[64]{0:T(128)S(1)}, f32[64]{0:T(128)}, u32[]{:S(2)}) copy-start(f32[64]{0:T(128)} %copy-done.39) | copy-start | bytes 772
  617.3 18.7 %copy-start.43 = (f32[64]{0:T(128)S(1)}, f32[64]{0:T(128)}, u32[]{:S(2)}) copy-start(f32[64]{0:T(128)} %copy-done.42) | copy-start | bytes 772
  617.3 18.7 %copy-start.45 = (f32[64]{0:T(128)S(1)}, f32[64]{0:T(128)}, u32[]{:S(2)}) copy-start(f32[64]{0:T(128)} %copy-done.44) | copy-start | bytes 772
  617.3 21.3 %copy-start.51 = (bf16[768,768]{1,0:T(8,128)(2,1)S(1)}, bf16[768,768]{1,0:T(8,128)(2,1)}, u32[]{:S(2)}) copy-start(bf16[768,768]{1,0:T(8,128)(2,1)} %param.23) | copy-start | bytes 3538948
  638.5 16.0 %copy-start.2 = (f32[12,512,512]{2,0,1:T(8,128)S(1)}, f32[12,512,512]{2,0,1:T(8,128)}, u32[]{:S(2)}) copy-start(f32[12,512,512]{2,0,1:T(8,128)} %copy.84) | copy-start | bytes 37748740
  654.5 17.5 %copy-start.8 = (bf16[1,2048,768]{2,1,0:T(8,128)(2,1)S(1)}, bf16[1,2048,768]{2,1,0:T(8,128)(2,1)}, u32[]{:S(2)}) copy-start(bf16[1,2048,768]{2,1,0:T(8,128)(2,1)} %param.18) | copy-start | bytes 9437188
  654.5 17.5 %copy-start.15 = (bf16[96,8,4,512]{3,1,2,0:T(8,128)(2,1)S(1)}, bf16[96,8,4,512]{3,1,2,0:T(8,128)(2,1)}, u32[]{:S(2)}) copy-start(bf16[96,8,4,512]{3,1,2,0:T(8,128)(2,1)} %copy-done.14) | copy-start | bytes 9437188
  672.1 48.7 %copy-start.30 = (f32[2048]{0:T(1024)S(1)}, f32[2048]{0:T(1024)}, u32[]{:S(2)}) copy-start(f32[2048]{0:T(1024)} %get-tuple-element.295) | copy-start | bytes 24580
  1055.9 10.7 slice-start.2
  (45 other events, 266.8 us)
Sparse Core Ops, SparseCore 0:
  617.4 432.2 all-reduce.3
where the time goes:
time: 1080 us
  matrix products  366 us (34%)
  waiting for transfers between devices  321 us (30%)
  local copies, waits for them, and re-layouts  153 us (14%)
  blocking collectives  112 us (10%)
  other arithmetic  109 us (10%)
  between operations  18 us (2%)
    psum x1, waiting for transfers between devices, local(): lax.psum((grad_attention, grad_query, grad_key, grad_value, grad_output,...  321 us
    all_gather x1, blocking collectives, local(): gathered = lax.all_gather(unit, ('tower', 'batch'), axis=0, tiled=True)  72.1 us
    dot_general x8, matrix products, score_block(): jnp.einsum('ihd,jhd->hij', query_rows, key_rows, preferred_element_type=j...  67.1 us
    convert_element_type x4, other arithmetic, attend_backward(): scores_low = grad_scores.astype(jnp.bfloat16)  65.7 us
    psum x1, blocking collectives, local(): lax.psum((grad_attention, grad_query, grad_key, grad_value, grad_output,...  39.6 us
    while x5, local copies, waits for them, and re-layouts, local(): lax.map(attend_forward, (query_all, key_all, value_all, valid))  35 us
    unnamed x132, local copies, waits for them, and re-layouts  34.2 us
    dot_general x4, matrix products, attend_backward(): jnp.einsum('ihd,jhd->hij', context_grad, value_rows, preferred_element_ty...  30 us
  transfers between devices with their start and end apart: 1, of which 1 were waited for; matrix products, arithmetic and copies ran while one was open for 7% of the time, Pallas kernels for 0%

commit v1 on v0

--- a/solution.py
+++ b/solution.py
@@ -1,3 +1,4 @@
+import functools
 import jax
 import jax.numpy as jnp
 from jax import lax
@@ -8,6 +9,25 @@
 score_scale = 100.0
 far_steps = (12, 16, 23, 32, 46, 64, 91)
 highest = lax.Precision.HIGHEST
+
+
+def guide_the_wall(arr_in, link_axis):
+    local_out = lax.psum(1, link_axis)
+    mat_out = lax.axis_index(link_axis)
+    current_value, z_new = (local_out, mat_out)
+    r_now, current_arr = (arr_in, 1)
+    while current_arr < current_value:
+        response = lax.ppermute(
+            r_now, link_axis, [(i0, i0 ^ current_arr) for i0 in range(current_value)]
+        )
+        y_new = jnp.concatenate([r_now, response], axis=0)
+        left_arr = jnp.concatenate([response, r_now], axis=0)
+        r_now = jnp.where(z_new & current_arr == 0, y_new, left_arr)
+        current_arr = 2 * current_arr
+    return r_now
+
+
+groups_pack = functools.partial(guide_the_wall, link_axis=("tower", "batch"))
 
 
 def bucket_onehot(slot_len, bucket_count):
@@ -108,7 +128,7 @@
     pooled = jnp.sum(final.reshape(seqs, slot_len, width) * pool_weight[:, :, None], axis=1)
     inverse_pool = lax.rsqrt(jnp.sum(pooled * pooled, axis=-1, keepdims=True) + epsilon)
     unit = pooled * inverse_pool
-    gathered = lax.all_gather(unit, ("tower", "batch"), axis=0, tiled=True)
+    gathered = groups_pack(unit)
     total_seqs = gathered.shape[0] // 2
     query_units = gathered[:total_seqs]
     doc_units = gathered[total_seqs:]

time: 1080 us -> 1040 us (0.963)
  blocking collectives: 112 us -> 42.3 us
  waiting for transfers between devices: 321 us -> 334 us
    all_gather x1 -> x0, blocking collectives: 72.1 us -> none  [local(): gathered = lax.all_gather(unit, ('tower', 'batch'), axis=0, tiled=True)]
    ppermute x0 -> x5, waiting for transfers between devices: none -> 10.8 us  [guide_the_wall(): lax.ppermute(r_now, link_axis, [(i0, i0 ^ current_arr) for i0 in range(cu...]
    unnamed x132 -> x140, local copies, waits for them, and re-layouts: 34.2 us -> 35.3 us
  transfers between devices with their start and end apart: 1 -> 6, of which waited for: 1 -> 6; matrix products, arithmetic and copies ran while one was open for 7% -> 7% of each run, Pallas kernels for 0% -> 0%
where the time goes in v1:
time: 1040 us; the launch traced here: 1030 us
  matrix products  366 us (35%)
  waiting for transfers between devices  334 us (32%)
  local copies, waits for them, and re-layouts  154 us (15%)
  other arithmetic  107 us (10%)
  blocking collectives  42.3 us (4%)
  between operations  18.1 us (2%)
  starting transfers between devices  10.8 us (1%)
    psum x1, waiting for transfers between devices, local(): lax.psum((grad_attention, grad_query, grad_key, grad_value, grad_output,...  323 us
    dot_general x8, matrix products, score_block(): jnp.einsum('ihd,jhd->hij', query_rows, key_rows, preferred_element_type=j...  67.1 us
    convert_element_type x4, other arithmetic, attend_backward(): scores_low = grad_scores.astype(jnp.bfloat16)  65.7 us
    psum x1, blocking collectives, local(): lax.psum((grad_attention, grad_query, grad_key, grad_value, grad_output,...  42.3 us
    while x5, local copies, waits for them, and re-layouts, local(): lax.map(attend_forward, (query_all, key_all, value_all, valid))  35.4 us
    unnamed x140, local copies, waits for them, and re-layouts  35.3 us
    dot_general x4, matrix products, attend_backward(): jnp.einsum('ihd,jhd->hij', context_grad, value_rows, preferred_element_ty...  30 us
    while x4, local copies, waits for them, and re-layouts, local(): lax.scan(attend_backward, jnp.zeros(bias.shape, jnp.float32), (query_all,...  27.5 us
  transfers between devices with their start and end apart: 6, of which 6 were waited for; matrix products, arithmetic and copies ran while one was open for 7% of the time, Pallas kernels for 0%

profile of v1, /device:TPU:0, one launch (start us, length us, event | category | flops | bytes accessed | tf_op | source)
XLA Modules:
  0.0 1032.5 jit_solution(5412967209169380705)
XLA Ops:
  74.4 13.6 %fusion.55 = f32[12,512,512]{2,0,1:T(8,128)} fusion(s32[512,512]{1,0:T(8,128)S(1)} %fusion.93, f32[32,12]{0,1:T(8,128)S(1)} %copy-done.38), kind=kOutput, calls=%fused_computation.65 | convolution fusion | flops 1216348160 | bytes 13633024 | tf_op jit(solution)/shard_map/ijb,bh->hij/dot_general | solution.py:85
  88.1 17.7 %copy.51 = f32[12,512,512]{1,2,0:T(8,128)} copy(f32[12,512,512]{2,0,1:T(8,128)} %fusion.55) | data formatting | bytes 25165824 | tf_op jit(solution)/shard_map/while | solution.py:117
  107.8 59.5 %while.29 = (s32[]{:T(128)}, bf16[4,512,12,64]{1,3,2,0:T(8,128)(2,1)}, f32[4,12,512]{2,1,0:T(8,128)}, bf16[4,512,12,64]{1,3,2,0:T(8,128)(2,1)}, pred[4,512]{1,0:...) while((s32[]{:T(128)}, ...), condition=%wide.region_4.5_spmd, body=%wide.region_1.4_spmd.sunk | while | flops 830859264 | bytes 53685868 | solution.py:117
  179.0 13.7 %fusion.117 = f32[2048,3072]{1,0:T(8,128)} fusion(bf16[768,3072]{1,0:T(8,128)(2,1)S(1)} %bitcast.266, f32[2048,768]{1,0:T(8,128)S(1)} %get-tuple-element.284, f32[768]{0:T(1024)S(1)} %copy-done.48, f32[2048]{0:T(1024)S(1)} %get-tuple-element.276), kind=kOutput, calls=%fused_computation.179 | convolution fusion | flops 9668395008 | bytes 36187136 | tf_op jit(solution)/shard_map/dot_general | solution.py:122
  192.8 18.1 %multiply_reduce_fusion.4 = (f32[2048]{0:T(1024)S(1)}, f32[2048,768]{1,0:T(8,128)}) fusion(f32[2048,768]{1,0:T(8,128)} %copy-done.16, bf16[3072,768]{1,0:T(8,128)(2,1)S(1)} %bitcast.264, f32[2048,3072]{1,0:T(8,128)} %fusion.117), kind=kOutput, calls=%fused_computation.101 | convolution fusion | flops 9687267328 | bytes 42475520 | tf_op jit(solution)/shard_map/dot_general | solution.py:124
  248.1 17.4 %fusion.83 = f32[3072,768]{1,0:T(8,128)} fusion(bf16[2048,768]{1,0:T(8,128)(2,1)S(1)} %fusion.82, f32[2048,3072]{1,0:T(8,128)} %fusion.117), kind=kOutput, calls=%fused_computation.110 | convolution fusion | flops 9682550784 | bytes 37748736 | tf_op jit(solution)/shard_map/tf,td->fd/dot_general | solution.py:164
  265.6 20.9 %fusion.52 = bf16[2048,3072]{1,0:T(8,128)(2,1)} fusion(f32[2048,3072]{1,0:T(8,128)} %fusion.117, bf16[2048,768]{1,0:T(8,128)(2,1)} %copy-done.22, bf16[3072,768]{1,0:T(8,128)(2,1)} %param.30), kind=kOutput, calls=%fused_computation.62 | convolution fusion | flops 9682550784 | bytes 45613056 | tf_op jit(solution)/shard_map/td,fd->tf/dot_general | solution.py:165
  286.5 19.3 %multiply_reduce_fusion.1 = (f32[768]{0:T(1024)}, f32[2048]{0:T(1024)S(1)}, f32[2048,768]{1,0:T(8,128)}) fusion(f32[2048,768]{1,0:T(8,128)} %copy-done.16, f32[2048]{0:T(1024)S(1)} %get-tuple-element.276, f32[768]{0:T(1024)S(1)} %copy-done.48, bf16[2048,3072]{1,0:T(8,128)(2,1)} %fusion.52, bf16[768,3072]{1,0:T(8,128)(2,1)} %param.29), kind=kOutput, calls=%fused_computation.95 | convolution fusion | flops 9673110528 | bytes 29906944 | tf_op jit(solution)/shard_map/tf,df->td/dot_general | solution.py:170
  305.8 15.6 %fusion.116 = f32[768,3072]{1,0:T(8,128)} fusion(bf16[2048,3072]{1,0:T(8,128)(2,1)} %fusion.52, f32[2048,768]{1,0:T(8,128)S(1)} %bitcast.248, f32[768]{0:T(1024)S(1)} %copy-done.48, f32[2048]{0:T(1024)S(1)} %get-tuple-element.276), kind=kOutput, calls=%fused_computation.178 | convolution fusion | flops 9668395008 | bytes 28322816 | tf_op jit(solution)/shard_map/td,tf->df/dot_general | solution.py:169
  354.8 183.0 %while.30 = (s32[]{:T(128)}, f32[12,512,512]{1,2,0:T(8,128)}, bf16[4,512,12,64]{1,3,2,0:T(8,128)(2,1)}, bf16[4,512,12,64]{1,3,2,0:T(8,128)(2,1)}, bf16[4,512,12,...) while((s32[]{:T(128)}, f32[12,512,512]{1,2,0:T(8,128)}, ...), condition=%wide.region_22.23_spmd.clone, body=%wide.region_20.22_spmd.clone.sunk | while | flops 2049042432 | bytes 177863392 | solution.py:214
  355.6 8.8 subtract_exponential_fusion.5
  374.8 13.5 %fusion.187 = (bf16[12,512,512]{1,2,0:T(8,128)(2,1)}, f32[12,512,512]{1,2,0:T(8,128)}) fusion(f32[12,512,512]{1,2,0:T(8,128)S(1)} %subtract_exponential_fusion.5, f32[12,512,512]{1,2,0:T(8,128)} %get-tuple-element.424, f32[12,512]{1,0:T(8,128)S(1)} %get-tuple-element.425, f32[12,512,512]{1,2,0:T(8,128)} %get-tuple-element.470, pred[]{:T(512)S(6)} %compare.3), kind=kLoop, calls=%fused_computation.24.clone.1 | loop fusion | flops 15728640 | bytes 56647680 | tf_op jit(solution)/shard_map/while/body/eval_jaxpr/convert_element_type | solution.py:198
  398.3 8.8 subtract_exponential_fusion.5
  417.5 17.4 %fusion.187 = (bf16[12,512,512]{1,2,0:T(8,128)(2,1)}, f32[12,512,512]{1,2,0:T(8,128)}) fusion(f32[12,512,512]{1,2,0:T(8,128)S(1)} %subtract_exponential_fusion.5, f32[12,512,512]{1,2,0:T(8,128)} %get-tuple-element.424, f32[12,512]{1,0:T(8,128)S(1)} %get-tuple-element.425, f32[12,512,512]{1,2,0:T(8,128)} %get-tuple-element.470, pred[]{:T(512)S(6)} %compare.3), kind=kLoop, calls=%fused_computation.24.clone.1 | loop fusion | flops 15728640 | bytes 56647680 | tf_op jit(solution)/shard_map/while/body/eval_jaxpr/convert_element_type | solution.py:198
  444.9 8.8 subtract_exponential_fusion.5
  464.2 17.4 %fusion.187 = (bf16[12,512,512]{1,2,0:T(8,128)(2,1)}, f32[12,512,512]{1,2,0:T(8,128)}) fusion(f32[12,512,512]{1,2,0:T(8,128)S(1)} %subtract_exponential_fusion.5, f32[12,512,512]{1,2,0:T(8,128)} %get-tuple-element.424, f32[12,512]{1,0:T(8,128)S(1)} %get-tuple-element.425, f32[12,512,512]{1,2,0:T(8,128)} %get-tuple-element.470, pred[]{:T(512)S(6)} %compare.3), kind=kLoop, calls=%fused_computation.24.clone.1 | loop fusion | flops 15728640 | bytes 56647680 | tf_op jit(solution)/shard_map/while/body/eval_jaxpr/convert_element_type | solution.py:198
  491.6 8.8 subtract_exponential_fusion.5
  510.9 17.4 %fusion.187 = (bf16[12,512,512]{1,2,0:T(8,128)(2,1)}, f32[12,512,512]{1,2,0:T(8,128)}) fusion(f32[12,512,512]{1,2,0:T(8,128)S(1)} %subtract_exponential_fusion.5, f32[12,512,512]{1,2,0:T(8,128)} %get-tuple-element.424, f32[12,512]{1,0:T(8,128)S(1)} %get-tuple-element.425, f32[12,512,512]{1,2,0:T(8,128)} %get-tuple-element.470, pred[]{:T(512)S(6)} %compare.3), kind=kLoop, calls=%fused_computation.24.clone.1 | loop fusion | flops 15728640 | bytes 56647680 | tf_op jit(solution)/shard_map/while/body/eval_jaxpr/convert_element_type | solution.py:198
  566.3 18.1 %copy.62 = f32[12,512,512]{2,0,1:T(8,128)} copy(f32[12,512,512]{1,2,0:T(8,128)} %get-tuple-element.126) | data formatting | bytes 25165824 | tf_op jit(solution)/shard_map/while | solution.py:214
  603.0 17.5 %fusion.92 = f32[32,12]{0,1:T(8,128)S(1)} fusion(f32[12,512,512]{2,0,1:T(8,128)S(1)} %copy-done.2, s32[512,512]{1,0:T(8,128)S(1)} %copy-done.11), kind=kOutput, calls=%fused_computation.121 | convolution fusion | flops 1216348160 | bytes 13633024 | tf_op jit(solution)/shard_map/ijb,hij->bh/dot_general | solution.py:222
  620.6 9.4 fusion.71
  630.0 42.3 %all-reduce = (f32[768]{0:T(1024)}, f32[32,12]{0,1:T(8,128)}, f32[768]{0:T(1024)}, f32[768]{0:T(1024)}) all-reduce(f32[768]{0:T(1024)S(1)} %get-tuple-element.208, f32[32,12]{0,1:T(8,128)S(1)} %fusion.92, f32[768]{0:T(1024)S(1)} %copy-done.49, f32[768]{0:T(1024)S(1)} %copy-done.35), channel_id=1, replica_groups=mesh['tower'=2,'batch'=16] {'tower','batch'}, use_global_device_ids=true, to_apply=%region_25.26 | all-reduce | flops 2688 | bytes 21504 | tf_op jit(solution)/shard_map/psum | solution.py:246
  680.6 323.0 %all-reduce.4.cloned.1.call-done = (f32[768,768]{1,0:T(8,128)}, f32[768,768]{1,0:T(8,128)}, f32[768,768]{1,0:T(8,128)}, f32[768,768]{1,0:T(8,128)}, f32[768,3072]{1,0:T(8,128)}, /*index=5*/f32[3072,768]{1,0:T(8,128)}) async-done(((f32[768,768]{1,0:T(8,128)}, f32[768,768]{1,0:T(8,128)}, f32[768,768]{1,0:T(8,128)}, f32[768,768]{1,0:T(8,128)}, f32[768,3072]{1,0:T(8,128)}, /*index=5*/f32[3072,768]{1,0:T(8,128)}), ...) | async-done | bytes 28311568 | tf_op jit(solution)/shard_map/psum | solution.py:246
  1011.3 9.3 copy.111
  (280 shorter events, 356.9 us)
Async XLA Ops:
  7.2 48.1 %copy-start = (bf16[768,768]{1,0:T(8,128)(2,1)S(1)}, bf16[768,768]{1,0:T(8,128)(2,1)}, u32[]{:S(2)}) copy-start(bf16[768,768]{1,0:T(8,128)(2,1)} %param.25) | copy-start | bytes 3538948
  7.2 996.5 %all-reduce.4.cloned.1.call-start = ((), (), s32[]{:S(2)}) async-start(), calls=%async_computation | async-start | bytes 56623104 | tf_op jit(solution)/shard_map/psum | solution.py:246
  7.7 66.8 %copy-start.10 = (s32[512,512]{1,0:T(8,128)}, s32[512,512]{1,0:T(8,128)S(1)}, u32[]{:S(2)}) copy-start(s32[512,512]{1,0:T(8,128)S(1)} %fusion.93) | copy-start | bytes 3145732
  12.5 42.8 %copy-start.29 = (f32[2048]{0:T(1024)}, f32[2048]{0:T(1024)S(1)}, u32[]{:S(2)}) copy-start(f32[2048]{0:T(1024)S(1)} %get-tuple-element.274) | copy-start | bytes 24580
  173.0 19.8 %slice-start.7 = ((s8[4718592]{0:T(1024)(128)(4,1)}), s8[4194304]{0:T(1024)(128)(4,1)S(1)}, s32[]{:S(2)}) async-start(s8[4718592]{0:T(1024)(128)(4,1)} %bitcast.263), calls=%async_computation.8 | async-start | bytes 8388608
  192.8 18.1 %copy-start.31 = (f32[768]{0:T(1024)S(1)}, f32[768]{0:T(1024)}, u32[]{:S(2)}) copy-start(f32[768]{0:T(1024)} %param.31) | copy-start | bytes 9220
  192.8 18.1 %copy-start.33 = (f32[4,512]{1,0:T(4,128)S(1)}, f32[4,512]{1,0:T(4,128)}, u32[]{:S(2)}) copy-start(f32[4,512]{1,0:T(4,128)} %get-tuple-element.280) | copy-start | bytes 24580
  210.9 24.9 %copy-start.34 = (f32[1,4,4,128]{3,2,1,0:T(4,128)S(1)}, f32[1,4,4,128]{3,2,1,0:T(4,128)}, u32[]{:S(2)}) copy-start(f32[1,4,4,128]{3,2,1,0:T(4,128)} %get-tuple-element.279) | copy-start | bytes 24580
  210.9 28.0 %copy-start.50 = (s32[64]{0:T(128)S(1)}, s32[64]{0:T(128)}, u32[]{:S(2)}) copy-start(s32[64]{0:T(128)} %param.21) | copy-start | bytes 772
  210.9 33.9 %slice-start = ((s8[6291456]{0:T(1024)(128)(4,1)}), s8[2097152]{0:T(1024)(128)(4,1)S(1)}, s32[]{:S(2)}) async-start(s8[6291456]{0:T(1024)(128)(4,1)} %bitcast.237), calls=%async_computation.1 | async-start | bytes 4194304
  214.6 4.6 collective-permute-start
  219.2 3.9 collective-permute-start.1
  223.2 4.1 collective-permute-start.2
  227.3 7.3 collective-permute-start.3
  235.7 1.6 collective-permute-start.4
  265.6 40.2 %slice-start.5 = ((s8[6291456]{0:T(1024)(128)(4,1)}), s8[2097152]{0:T(1024)(128)(4,1)S(1)}, s32[]{:S(2)}) async-start(s8[6291456]{0:T(1024)(128)(4,1)} %bitcast.247), calls=%async_computation.6 | async-start | bytes 4194304
  286.5 19.3 %slice-start.6 = ((s8[6291456]{0:T(1024)(128)(4,1)}), s8[4194304]{0:T(1024)(128)(4,1)S(1)}, s32[]{:S(2)}) async-start(s8[6291456]{0:T(1024)(128)(4,1)} %bitcast.247), calls=%async_computation.7 | async-start | bytes 8388608
  566.2 18.2 %copy-start.40 = (f32[64]{0:T(128)S(1)}, f32[64]{0:T(128)}, u32[]{:S(2)}) copy-start(f32[64]{0:T(128)} %copy-done.39) | copy-start | bytes 772
  566.2 18.1 %copy-start.42 = (f32[64]{0:T(128)S(1)}, f32[64]{0:T(128)}, u32[]{:S(2)}) copy-start(f32[64]{0:T(128)} %copy-done.41) | copy-start | bytes 772
  566.3 18.1 %copy-start.45 = (f32[64]{0:T(128)S(1)}, f32[64]{0:T(128)}, u32[]{:S(2)}) copy-start(f32[64]{0:T(128)} %copy-done.44) | copy-start | bytes 772
  566.3 18.1 %copy-start.47 = (f32[64]{0:T(128)S(1)}, f32[64]{0:T(128)}, u32[]{:S(2)}) copy-start(f32[64]{0:T(128)} %copy-done.46) | copy-start | bytes 772
  566.3 20.7 %copy-start.53 = (bf16[768,768]{1,0:T(8,128)(2,1)S(1)}, bf16[768,768]{1,0:T(8,128)(2,1)}, u32[]{:S(2)}) copy-start(bf16[768,768]{1,0:T(8,128)(2,1)} %param.23) | copy-start | bytes 3538948
  603.0 17.5 %copy-start.15 = (bf16[96,8,4,512]{3,1,2,0:T(8,128)(2,1)S(1)}, bf16[96,8,4,512]{3,1,2,0:T(8,128)(2,1)}, u32[]{:S(2)}) copy-start(bf16[96,8,4,512]{3,1,2,0:T(8,128)(2,1)} %copy-done.14) | copy-start | bytes 9437188
  620.6 51.7 %copy-start.32 = (f32[2048]{0:T(1024)S(1)}, f32[2048]{0:T(1024)}, u32[]{:S(2)}) copy-start(f32[2048]{0:T(1024)} %get-tuple-element.273) | copy-start | bytes 24580
  (54 other events, 375.5 us)
Sparse Core Ops, SparseCore 0:
  566.4 437.2 all-reduce.3
